TPU v7x, 32 devices: a whole 2x2x4 slice. The times are simulated.
32 devices in a mesh: dp: 16 (over z, y, x), tensor: 2 (over core).
Axes of the slice: x: 2, y: 2, z: 4, core: 2. Of those that a mesh axis runs over, the one named last changes fastest.
Arguments:
- tokens: bfloat16 [4096, 768], P(('dp', 'tensor')), may hold values from -6 to 6
- segments: int32 [4096], P('dp'), may hold values from 0 to 7, as said below
- attention_gain: float32 [768], replicated, may hold values from 0.1 to 1.9
- attention_shift: float32 [768], replicated, may hold values from -3 to 3
- query_key_value: bfloat16 [768, 3, 768], P(None, None, 'tensor'), may hold values from -0.21875 to 0.21875
- query_value_bias: float32 [2, 768], P(None, 'tensor'), may hold values from -3 to 3
- output_weight: bfloat16 [768, 768], P('tensor'), may hold values from -0.875 to 0.875
- output_bias: float32 [768], replicated, may hold values from -3 to 3
- feedforward_gain: float32 [768], replicated, may hold values from 0.1 to 1.9
- feedforward_shift: float32 [768], replicated, may hold values from -3 to 3
- expand_weight: bfloat16 [768, 3072], P(None, 'tensor'), may hold values from -0.21875 to 0.21875
- expand_bias: float32 [3072], P('tensor'), may hold values from -3 to 3
- contract_weight: bfloat16 [3072, 768], P('tensor'), may hold values from -0.21875 to 0.21875
- contract_bias: float32 [768], replicated, may hold values from -3 to 3
- cotangent: bfloat16 [4096, 768], P(('dp', 'tensor')), may hold values from -6 to 6
Outputs:
- block_output: float32 [4096, 768], P(('dp', 'tensor'))
- input_gradient: float32 [4096, 768], P(('dp', 'tensor'))
- attention_gain_gradient: float32 [768], replicated
- attention_shift_gradient: float32 [768], replicated
- query_key_value_gradient: float32 [768, 3, 768], P('dp', None, 'tensor')
- query_value_bias_gradient: float32 [2, 768], P(None, 'tensor')
- output_weight_gradient: float32 [768, 768], P('tensor', 'dp')
- output_bias_gradient: float32 [768], replicated
- feedforward_gain_gradient: float32 [768], replicated
- feedforward_shift_gradient: float32 [768], replicated
- expand_weight_gradient: float32 [768, 3072], P('dp', 'tensor')
- expand_bias_gradient: float32 [3072], P('tensor')
- contract_weight_gradient: float32 [3072, 768], P('tensor', 'dp')
- contract_bias_gradient: float32 [768], replicated
Inputs may be any that keep to these rules, and one draw needn't show every extreme that they name: `segments`: within each pack of 256 tokens the numbers start at 0, never fall and rise by at most one from token to token; a sequence is a run of one number in one pack and holds 1 to 256 tokens; some sequence holds exactly 256; some pack holds 8 sequences.
All inputs are finite; a program needn't handle non-finite values.
Results may differ from a plain program's by a relative error of at most 0.012.
The roundings to bfloat16 on the way count: a program that leaves them out, or rounds other values in their place, can miss the bound.
Values may be sent and summed in bfloat16 or wider, within the bound.
A program may use at most 128 MiB of HBM per device.

v0:
```python
import jax
import jax.numpy as jnp
from jax import lax
from jax.sharding import PartitionSpec as P

HEAD_DIM = 64
epsilon = 1e-05


def normalize(values, gain, shift):
    center = jnp.mean(values, axis=-1, keepdims=True)
    centered = values - center
    spread = jnp.mean(centered * centered, axis=-1, keepdims=True)
    inverse = lax.rsqrt(spread + epsilon)
    unit = centered * inverse
    return (unit * gain + shift, unit, inverse)


def normalize_back(unit, inverse, gain, incoming):
    scaled = incoming * gain
    first = jnp.mean(scaled, axis=-1, keepdims=True)
    second = jnp.mean(scaled * unit, axis=-1, keepdims=True)
    return inverse * (scaled - first - unit * second)


def gelu_tanh(values):
    return jax.nn.gelu(values, approximate=True)


def allowed_pairs(segments):
    count = segments.shape[0]
    query_place = lax.broadcasted_iota(jnp.int32, (count, count), 0)
    key_place = lax.broadcasted_iota(jnp.int32, (count, count), 1)
    return (key_place <= query_place) & (segments[:, None] == segments[None, :])


def contract_rows(left, right):
    return lax.dot_general(
        left, right, (((0,), (0,)), ((), ())), preferred_element_type=jnp.float32
    )


def contract_columns(left, right):
    return lax.dot_general(
        left, right, (((1,), (1,)), ((), ())), preferred_element_type=jnp.float32
    )


def attention_weights(query, keys, allowed, scale, log_total):
    scores = jnp.einsum("qhe,khe->hqk", query, keys, preferred_element_type=jnp.float32) * scale
    masked = jnp.where(allowed, scores, -1e30)
    return jnp.where(allowed, jnp.exp(masked - log_total), 0.0)


def shards(
    tokens,
    segments,
    attention_gain,
    attention_shift,
    query_key_value,
    query_value_bias,
    output_weight,
    output_bias,
    feedforward_gain,
    feedforward_shift,
    expand_weight,
    expand_bias,
    contract_weight,
    contract_bias,
    cotangent,
):
    width = tokens.shape[1]
    local = query_key_value.shape[2]
    heads_here = local // HEAD_DIM
    scale = HEAD_DIM ** (-0.5)
    flat_weight = query_key_value.reshape(width, 3 * local)
    residual_in = tokens.astype(jnp.float32)
    normed_share, unit_one, inverse_one = normalize(residual_in, attention_gain, attention_shift)
    normed_share = normed_share.astype(jnp.bfloat16)
    normed_one, cotangent_rows = (
        lax.all_gather(normed_share, "tensor", axis=0, tiled=True),
        lax.all_gather(cotangent, "tensor", axis=0, tiled=True),
    )
    length = normed_one.shape[0]
    joined = jnp.dot(normed_one, flat_weight, preferred_element_type=jnp.float32).reshape(
        length, 3, local
    )
    query = (
        (joined[:, 0] + query_value_bias[0])
        .astype(jnp.bfloat16)
        .reshape(length, heads_here, HEAD_DIM)
    )
    keys = joined[:, 1].astype(jnp.bfloat16).reshape(length, heads_here, HEAD_DIM)
    values = (
        (joined[:, 2] + query_value_bias[1])
        .astype(jnp.bfloat16)
        .reshape(length, heads_here, HEAD_DIM)
    )
    allowed = allowed_pairs(segments)[None]
    scores = jnp.einsum("qhe,khe->hqk", query, keys, preferred_element_type=jnp.float32) * scale
    masked = jnp.where(allowed, scores, -1e30)
    highest = jnp.max(masked, axis=2, keepdims=True)
    log_total = highest + jnp.log(jnp.sum(jnp.exp(masked - highest), axis=2, keepdims=True))
    weights_low = jnp.where(allowed, jnp.exp(masked - log_total), 0.0).astype(jnp.bfloat16)
    mixed = jnp.einsum("hqk,khe->qhe", weights_low, values, preferred_element_type=jnp.float32)
    mixed = mixed.astype(jnp.bfloat16)
    mixed_flat = mixed.reshape(length, local)
    partial_attention = jnp.dot(mixed_flat, output_weight, preferred_element_type=jnp.float32)
    attention_share = lax.psum_scatter(partial_attention, "tensor", scatter_dimension=0, tiled=True)
    hidden = residual_in + attention_share + output_bias
    normed_two_share, unit_two, inverse_two = normalize(hidden, feedforward_gain, feedforward_shift)
    normed_two = lax.all_gather(normed_two_share.astype(jnp.bfloat16), "tensor", axis=0, tiled=True)
    before = jnp.dot(normed_two, expand_weight, preferred_element_type=jnp.float32) + expand_bias
    after, gelu_back = jax.vjp(gelu_tanh, before)
    after_low = after.astype(jnp.bfloat16)
    partial_feed = jnp.dot(after_low, contract_weight, preferred_element_type=jnp.float32)
    block_output = (
        hidden
        + lax.psum_scatter(partial_feed, "tensor", scatter_dimension=0, tiled=True)
        + contract_bias
    )
    upstream = cotangent.astype(jnp.float32)
    contract_bias_grad = jnp.sum(upstream, axis=0)
    contract_grad = contract_rows(after_low, cotangent_rows)
    d_after = contract_columns(cotangent_rows, contract_weight)
    d_before = gelu_back(d_after)[0]
    expand_bias_grad = jnp.sum(d_before, axis=0)
    d_before_low = d_before.astype(jnp.bfloat16)
    expand_grad = contract_rows(normed_two, d_before_low)
    partial_second = contract_columns(d_before_low, expand_weight)
    d_normed_two = lax.psum_scatter(partial_second, "tensor", scatter_dimension=0, tiled=True)
    feed_gain_grad = jnp.sum(d_normed_two * unit_two, axis=0)
    feed_shift_grad = jnp.sum(d_normed_two, axis=0)
    d_hidden = upstream + normalize_back(unit_two, inverse_two, feedforward_gain, d_normed_two)
    output_bias_grad = jnp.sum(d_hidden, axis=0)
    d_hidden_low = lax.all_gather(d_hidden.astype(jnp.bfloat16), "tensor", axis=0, tiled=True)
    output_grad = contract_rows(mixed_flat, d_hidden_low)
    d_mixed = contract_columns(d_hidden_low, output_weight).astype(jnp.bfloat16)
    d_mixed = d_mixed.reshape(length, heads_here, HEAD_DIM)
    weights = attention_weights(query, keys, allowed, scale, log_total)
    weights_again = weights.astype(jnp.bfloat16)
    d_weights = jnp.einsum("qhe,khe->hqk", d_mixed, values, preferred_element_type=jnp.float32)
    delta = jnp.einsum("qhe,qhe->hq", d_mixed, mixed, preferred_element_type=jnp.float32)
    d_scores = (weights * (d_weights - delta[:, :, None]) * scale).astype(jnp.bfloat16)
    d_values = jnp.einsum(
        "hqk,qhe->khe", weights_again, d_mixed, preferred_element_type=jnp.float32
    )
    d_query = jnp.einsum("hqk,khe->qhe", d_scores, keys, preferred_element_type=jnp.float32)
    d_keys = jnp.einsum("hqk,qhe->khe", d_scores, query, preferred_element_type=jnp.float32)
    d_query = d_query.reshape(length, local)
    d_keys = d_keys.reshape(length, local)
    d_values = d_values.reshape(length, local)
    bias_grad = jnp.stack([jnp.sum(d_query, axis=0), jnp.sum(d_values, axis=0)])
    d_joined_low = (
        jnp.stack([d_query, d_keys, d_values], axis=1)
        .astype(jnp.bfloat16)
        .reshape(length, 3 * local)
    )
    joined_grad = contract_rows(normed_one, d_joined_low).reshape(width, 3, local)
    partial_first = contract_columns(d_joined_low, flat_weight)
    d_normed_one = lax.psum_scatter(partial_first, "tensor", scatter_dimension=0, tiled=True)
    first_gain_grad = jnp.sum(d_normed_one * unit_one, axis=0)
    first_shift_grad = jnp.sum(d_normed_one, axis=0)
    input_gradient = d_hidden + normalize_back(unit_one, inverse_one, attention_gain, d_normed_one)
    joined_share, output_share, expand_share, contract_share = (
        lax.psum_scatter(joined_grad, "dp", scatter_dimension=0, tiled=True),
        lax.psum_scatter(output_grad, "dp", scatter_dimension=1, tiled=True),
        lax.psum_scatter(expand_grad, "dp", scatter_dimension=0, tiled=True),
        lax.psum_scatter(contract_grad, "dp", scatter_dimension=1, tiled=True),
    )
    row_sums = lax.psum(
        (
            first_gain_grad,
            first_shift_grad,
            output_bias_grad,
            feed_gain_grad,
            feed_shift_grad,
            contract_bias_grad,
        ),
        ("dp", "tensor"),
    )
    unit_sums = lax.psum((bias_grad, expand_bias_grad), "dp")
    return (
        block_output,
        input_gradient,
        row_sums[0],
        row_sums[1],
        joined_share,
        unit_sums[0],
        output_share,
        row_sums[2],
        row_sums[3],
        row_sums[4],
        expand_share,
        unit_sums[1],
        contract_share,
        row_sums[5],
    )


def solution(mesh):
    in_specs = (
        P(("dp", "tensor"), None),
        P("dp"),
        P(),
        P(),
        P(None, None, "tensor"),
        P(None, "tensor"),
        P("tensor", None),
        P(),
        P(),
        P(),
        P(None, "tensor"),
        P("tensor"),
        P("tensor", None),
        P(),
        P(("dp", "tensor"), None),
    )
    out_specs = (
        P(("dp", "tensor"), None),
        P(("dp", "tensor"), None),
        P(),
        P(),
        P("dp", None, "tensor"),
        P(None, "tensor"),
        P("tensor", "dp"),
        P(),
        P(),
        P(),
        P("dp", "tensor"),
        P("tensor"),
        P("tensor", "dp"),
        P(),
    )
    return jax.shard_map(shards, mesh=mesh, in_specs=in_specs, out_specs=out_specs, check_vma=False)
```

profile of v0, /device:TPU:0, one launch (start us, length us, event | category | flops | bytes accessed | tf_op | source)
XLA Modules:
  0.0 668.4 jit_solution(5672348374279710601)
XLA Ops:
  11.2 2.2 all_gather.12
  13.4 3.9 copy.44
  17.3 2.2 fusion
  28.0 2.1 all_gather.14
  30.9 3.7 fusion.50
  34.5 4.4 reduce-scatter.9.cloned.1.call-done
  41.2 2.1 all_gather.13
  43.4 3.5 fusion.42
  49.5 4.1 fusion.41
  53.7 5.2 reduce-scatter.13.cloned.1.call-done
  61.2 9.2 %reduce-scatter.11.cloned.1.call-done = f32[128,768]{1,0:T(8,128)} async-done(((f32[256,768]{1,0:T(8,128)}), f32[128,768]{1,0:T(8,128)}) %reduce-scatter.11.cloned.1.call-update) | async-done | bytes 393232 | tf_op jit(solution)/shard_map/reduce_scatter | solution.py:119
  70.4 2.9 fusion.44
  74.1 2.1 all_gather.15
  80.1 3.1 bitcast_reduce_fusion
  91.4 3.4 convolution_bitcast_fusion
  99.9 2.5 fusion.9
  103.4 4.5 fusion.40
  109.0 4.1 fusion.29
  113.9 77.1 %all-reduce.1 = (f32[2,384]{1,0:T(2,128)}, f32[1536]{0:T(1024)}) all-reduce(f32[2,384]{1,0:T(2,128)S(1)} %pad_maximum_fusion, f32[1536]{0:T(1024)S(1)} %copy-done.35), channel_id=1, replica_groups=mesh['dp'=16,'tensor'=2] {'dp'}, use_global_device_ids=true, to_apply=%region_21.22 | all-reduce | flops 2304 | bytes 18432 | tf_op jit(solution)/shard_map/psum | solution.py:182
  192.2 37.8 %all-reduce = (f32[768]{0:T(1024)}, f32[768]{0:T(1024)}, f32[768]{0:T(1024)}, f32[768]{0:T(1024)}, f32[768]{0:T(1024)}, /*index=5*/f32[768]{0:T(1024)}) all-reduce(f32[768]{0:T(1024)S(1)} %get-tuple-element.16, f32[768]{0:T(1024)S(1)} %get-tuple-element.21, ...), channel_id=1, replica_groups=mesh['dp'=16,'tensor'=2] {'dp','tensor'}, use_global_device_ids=true, to_apply=%region_15.16 | all-reduce | flops 4608 | bytes 36864 | tf_op jit(solution)/shard_map/psum | solution.py:171
  231.9 3.8 reduce-scatter.19.cloned.1.call-done
  235.7 139.6 %reduce-scatter.17.cloned.1.call-done = f32[48,3,384]{2,0,1:T(8,128)} async-done(((f32[768,3,384]{2,0,1:T(8,128)}), f32[48,3,384]{2,0,1:T(8,128)}) %reduce-scatter.17.cloned.1.call-update) | async-done | bytes 221200 | tf_op jit(solution)/shard_map/reduce_scatter | solution.py:166
  375.3 143.1 %reduce-scatter.23.cloned.1.call-done = f32[1536,48]{0,1:T(8,128)} async-done(((f32[1536,768]{0,1:T(8,128)}), f32[1536,48]{0,1:T(8,128)}) %reduce-scatter.23.cloned.1.call-update) | async-done | bytes 294928 | tf_op jit(solution)/shard_map/reduce_scatter | solution.py:169
  518.4 143.2 %reduce-scatter.21.cloned.1.call-done = f32[48,1536]{1,0:T(8,128)} async-done(((f32[768,1536]{1,0:T(8,128)}), f32[48,1536]{1,0:T(8,128)}) %reduce-scatter.21.cloned.1.call-update) | async-done | bytes 294928 | tf_op jit(solution)/shard_map/reduce_scatter | solution.py:168
  (150 shorter events, 44.3 us)
Async XLA Ops:
  7.2 36.2 %copy-start = (bf16[768,1536]{1,0:T(8,128)(2,1)S(1)}, bf16[768,1536]{1,0:T(8,128)(2,1)}, u32[]{:S(2)}) copy-start(bf16[768,1536]{1,0:T(8,128)(2,1)} %param.25) | copy-start | bytes 7077892
  7.2 31.7 %reduce-scatter.9.cloned.1.call-start = ((), (), s32[]{:S(2)}) async-start(), calls=%async_computation.8 | async-start | bytes 1179648 | tf_op jit(solution)/shard_map/reduce_scatter | solution.py:109
  20.5 5.0 copy-start.26
  28.0 30.9 %reduce-scatter.13.cloned.1.call-start = ((), (), s32[]{:S(2)}) async-start(), calls=%async_computation.10 | async-start | bytes 1179648 | tf_op jit(solution)/shard_map/reduce_scatter | solution.py:131
  30.9 8.0 %copy-start.3 = (bf16[128,768]{1,0:T(8,128)(2,1)S(1)}, bf16[128,768]{1,0:T(8,128)(2,1)}, u32[]{:S(2)}) copy-start(bf16[128,768]{1,0:T(8,128)(2,1)} %param.15) | copy-start | bytes 589828
  30.9 9.5 %copy-start.24 = (f32[768]{0:T(1024)S(1)}, f32[768]{0:T(1024)}, u32[]{:S(2)}) copy-start(f32[768]{0:T(1024)} %param.23) | copy-start | bytes 9220
  38.9 4.5 copy-start.16
  38.9 4.5 copy-start.42
  49.5 21.0 %reduce-scatter.11.cloned.1.call-start = ((), (), s32[]{:S(2)}) async-start(), calls=%async_computation.9 | async-start | bytes 1179648 | tf_op jit(solution)/shard_map/reduce_scatter | solution.py:119
  53.6 137.3 %reduce-scatter.15.cloned.1.call-start = ((), (), s32[]{:S(2)}) async-start(), calls=%async_computation.11 | async-start | bytes 1179648 | tf_op jit(solution)/shard_map/reduce_scatter | solution.py:161
  70.4 5.7 copy-start.11
  77.2 6.0 copy-start.27
  94.9 140.9 %reduce-scatter.19.cloned.1.call-start = ((), (), s32[]{:S(2)}) async-start(), calls=%async_computation.13 | async-start | bytes 1253376 | tf_op jit(solution)/shard_map/reduce_scatter | solution.py:167
  96.4 278.9 %reduce-scatter.17.cloned.1.call-start = ((), (), s32[]{:S(2)}) async-start(), calls=%async_computation.12 | async-start | bytes 3760128 | tf_op jit(solution)/shard_map/reduce_scatter | solution.py:166
  102.5 415.9 %reduce-scatter.23.cloned.1.call-start = ((), (), s32[]{:S(2)}) async-start(), calls=%async_computation.15 | async-start | bytes 5013504 | tf_op jit(solution)/shard_map/reduce_scatter | solution.py:169
  108.0 553.5 %reduce-scatter.21.cloned.1.call-start = ((), (), s32[]{:S(2)}) async-start(), calls=%async_computation.14 | async-start | bytes 5013504 | tf_op jit(solution)/shard_map/reduce_scatter | solution.py:168
  113.1 77.9 %copy-start.25 = (f32[768]{0:T(1024)S(1)}, f32[768]{0:T(1024)}, u32[]{:S(2)}) copy-start(f32[768]{0:T(1024)} %param.17) | copy-start | bytes 9220
  113.1 77.9 %copy-start.33 = (f32[128]{0:T(128)S(1)}, f32[128]{0:T(128)}, u32[]{:S(2)}) copy-start(f32[128]{0:T(128)} %copy-done.32) | copy-start | bytes 1540
  113.1 77.8 %copy-start.37 = (f32[128]{0:T(128)S(1)}, f32[128]{0:T(128)}, u32[]{:S(2)}) copy-start(f32[128]{0:T(128)} %copy-done.36) | copy-start | bytes 1540
  113.1 79.1 %copy-start.28 = (f32[768]{0:T(1024)S(1)}, f32[768]{0:T(1024)}, u32[]{:S(2)}) copy-start(f32[768]{0:T(1024)} %get-tuple-element.14) | copy-start | bytes 9220
  113.1 79.1 %copy-start.29 = (f32[768]{0:T(1024)S(1)}, f32[768]{0:T(1024)}, u32[]{:S(2)}) copy-start(f32[768]{0:T(1024)} %get-tuple-element.20) | copy-start | bytes 9220
  113.1 79.1 %copy-start.30 = (f32[768]{0:T(1024)S(1)}, f32[768]{0:T(1024)}, u32[]{:S(2)}) copy-start(f32[768]{0:T(1024)} %get-tuple-element.34) | copy-start | bytes 9220
  113.1 79.1 %copy-start.31 = (f32[768]{0:T(1024)S(1)}, f32[768]{0:T(1024)}, u32[]{:S(2)}) copy-start(f32[768]{0:T(1024)} %get-tuple-element.41) | copy-start | bytes 9220
  113.1 116.9 %copy-start.5 = (f32[128,768]{1,0:T(8,128)S(1)}, f32[128,768]{1,0:T(8,128)}, u32[]{:S(2)}) copy-start(f32[128,768]{1,0:T(8,128)} %copy-done.4) | copy-start | bytes 1179652
  (27 other events, 47.7 us)
Sparse Core Ops, SparseCore 0:
  28.1 10.7 reduce-scatter.8
  49.6 9.2 reduce-scatter.12
  61.1 9.2 reduce-scatter.10
  95.0 9.2 reduce-scatter.14
  109.5 126.1 reduce-scatter.18
  241.2 134.0 reduce-scatter.16
  381.0 137.2 reduce-scatter.22
  524.1 137.3 reduce-scatter.20
where the time goes:
time: 669 us; the launch traced here: 668 us
  waiting for transfers between devices  448 us (67%)
  blocking collectives  123 us (18%)
  matrix products  41.2 us (6%)
  local copies, waits for them, and re-layouts  22 us (3%)
  other arithmetic  18.3 us (3%)
  between operations  14.6 us (2%)
    reduce_scatter x1, waiting for transfers between devices, shards(): lax.psum_scatter(expand_grad, 'dp', scatter_dimension=0, tiled=True)  143 us
    reduce_scatter x1, waiting for transfers between devices, shards(): lax.psum_scatter(contract_grad, 'dp', scatter_dimension=1, tiled=True)  143 us
    reduce_scatter x1, waiting for transfers between devices, shards(): lax.psum_scatter(joined_grad, 'dp', scatter_dimension=0, tiled=True)  140 us
    psum x1, blocking collectives, shards(): unit_sums = lax.psum((bias_grad, expand_bias_grad), 'dp')  77.1 us
    psum x1, blocking collectives, shards(): lax.psum((first_gain_grad, first_shift_grad, output_bias_grad, feed_gain_...  37.8 us
  transfers between devices with their start and end apart: 8, of which 7 were waited for; matrix products, arithmetic and copies ran while one was open for 4% of the time, Pallas kernels for 0%

commit v1 on v0

--- a/solution.py
+++ b/solution.py
@@ -169,15 +169,18 @@
         lax.psum_scatter(contract_grad, "dp", scatter_dimension=1, tiled=True),
     )
     row_sums = lax.psum(
-        (
-            first_gain_grad,
-            first_shift_grad,
-            output_bias_grad,
-            feed_gain_grad,
-            feed_shift_grad,
-            contract_bias_grad,
+        lax.psum(
+            (
+                first_gain_grad,
+                first_shift_grad,
+                output_bias_grad,
+                feed_gain_grad,
+                feed_shift_grad,
+                contract_bias_grad,
+            ),
+            "tensor",
         ),
-        ("dp", "tensor"),
+        "dp",
     )
     unit_sums = lax.psum((bias_grad, expand_bias_grad), "dp")
     return (

time: 669 us -> 668 us (level)
  waiting for transfers between devices: 448 us -> 482 us
  blocking collectives: 123 us -> 89.7 us
    psum x1, blocking collectives: 37.8 us -> 3.44 us  [shards(): lax.psum((first_gain_grad, first_shift_grad, output_bias_grad, feed_gain_...]
    reduce_scatter x1, waiting for transfers between devices: 3.77 us -> 37.3 us  [shards(): lax.psum_scatter(output_grad, 'dp', scatter_dimension=1, tiled=True)]
where the time goes in v1:
time: 668 us; the launch traced here: 667 us
  waiting for transfers between devices  482 us (72%)
  blocking collectives  89.7 us (13%)
  matrix products  41.3 us (6%)
  local copies, waits for them, and re-layouts  20.8 us (3%)
  other arithmetic  18.3 us (3%)
  between operations  14.7 us (2%)
    reduce_scatter x1, waiting for transfers between devices, shards(): lax.psum_scatter(expand_grad, 'dp', scatter_dimension=0, tiled=True)  143 us
    reduce_scatter x1, waiting for transfers between devices, shards(): lax.psum_scatter(contract_grad, 'dp', scatter_dimension=1, tiled=True)  143 us
    reduce_scatter x1, waiting for transfers between devices, shards(): lax.psum_scatter(joined_grad, 'dp', scatter_dimension=0, tiled=True)  139 us
    psum x1, blocking collectives, shards(): lax.psum(lax.psum((first_gain_grad, first_shift_grad, output_bias_grad, f...  77.8 us
    reduce_scatter x1, waiting for transfers between devices, shards(): lax.psum_scatter(output_grad, 'dp', scatter_dimension=1, tiled=True)  37.3 us
  transfers between devices with their start and end apart: 8, of which 7 were waited for; matrix products, arithmetic and copies ran while one was open for 4% of the time, Pallas kernels for 0%

profile of v1, /device:TPU:0, one launch (start us, length us, event | category | flops | bytes accessed | tf_op | source)
XLA Modules:
  0.0 667.0 jit_solution(15860452528496530177)
XLA Ops:
  10.7 2.2 all_gather.12
  12.9 3.9 copy.44
  16.8 2.2 fusion
  27.5 2.1 all_gather.14
  29.6 3.8 fusion.50
  33.4 5.0 reduce-scatter.9.cloned.1.call-done
  40.8 2.1 all_gather.13
  42.9 3.5 fusion.42
  49.0 4.1 fusion.41
  53.2 5.2 reduce-scatter.13.cloned.1.call-done
  60.8 9.2 %reduce-scatter.11.cloned.1.call-done = f32[128,768]{1,0:T(8,128)} async-done(((f32[256,768]{1,0:T(8,128)}), f32[128,768]{1,0:T(8,128)}) %reduce-scatter.11.cloned.1.call-update) | async-done | bytes 393232 | tf_op jit(solution)/shard_map/reduce_scatter | solution.py:119
  70.0 2.9 fusion.44
  73.6 2.1 all_gather.15
  79.7 3.1 bitcast_reduce_fusion
  91.0 3.4 convolution_bitcast_fusion
  99.5 2.5 fusion.9
  103.0 4.5 fusion.40
  108.5 4.1 fusion.29
  114.7 3.4 all-reduce.1
  118.2 77.8 %all-reduce = (f32[768]{0:T(1024)}, f32[768]{0:T(1024)}, f32[2,384]{1,0:T(2,128)}, f32[768]{0:T(1024)}, f32[768]{0:T(1024)}, /*index=5*/f32[768]{0:T(1024)}, f32[1536]{0:T(1024)}, f32[768]{0:T(1024)}) all-reduce(f32[768]{0:T(1024)S(1)} %get-tuple-element.32, ...), channel_id=1, replica_groups=mesh['dp'=16,'tensor'=2] {'dp'}, use_global_device_ids=true, to_apply=%region_16.17 | all-reduce | flops 6912 | bytes 55296 | tf_op jit(solution)/shard_map/psum | solution.py:171
  197.9 37.3 %reduce-scatter.19.cloned.1.call-done = f32[384,48]{0,1:T(8,128)} async-done(((f32[384,768]{0,1:T(8,128)}), f32[384,48]{0,1:T(8,128)}) %reduce-scatter.19.cloned.1.call-update) | async-done | bytes 73744 | tf_op jit(solution)/shard_map/reduce_scatter | solution.py:167
  235.2 139.0 %reduce-scatter.17.cloned.1.call-done = f32[48,3,384]{2,0,1:T(8,128)} async-done(((f32[768,3,384]{2,0,1:T(8,128)}), f32[48,3,384]{2,0,1:T(8,128)}) %reduce-scatter.17.cloned.1.call-update) | async-done | bytes 221200 | tf_op jit(solution)/shard_map/reduce_scatter | solution.py:166
  374.2 142.6 %reduce-scatter.23.cloned.1.call-done = f32[1536,48]{0,1:T(8,128)} async-done(((f32[1536,768]{0,1:T(8,128)}), f32[1536,48]{0,1:T(8,128)}) %reduce-scatter.23.cloned.1.call-update) | async-done | bytes 294928 | tf_op jit(solution)/shard_map/reduce_scatter | solution.py:169
  516.9 143.3 %reduce-scatter.21.cloned.1.call-done = f32[48,1536]{1,0:T(8,128)} async-done(((f32[768,1536]{1,0:T(8,128)}), f32[48,1536]{1,0:T(8,128)}) %reduce-scatter.21.cloned.1.call-update) | async-done | bytes 294928 | tf_op jit(solution)/shard_map/reduce_scatter | solution.py:168
  (150 shorter events, 43.1 us)
Async XLA Ops:
  7.2 35.7 %copy-start = (bf16[768,1536]{1,0:T(8,128)(2,1)S(1)}, bf16[768,1536]{1,0:T(8,128)(2,1)}, u32[]{:S(2)}) copy-start(bf16[768,1536]{1,0:T(8,128)(2,1)} %param.25) | copy-start | bytes 7077892
  7.2 31.2 %reduce-scatter.9.cloned.1.call-start = ((), (), s32[]{:S(2)}) async-start(), calls=%async_computation.8 | async-start | bytes 1179648 | tf_op jit(solution)/shard_map/reduce_scatter | solution.py:109
  20.0 5.0 copy-start.26
  27.5 30.9 %reduce-scatter.13.cloned.1.call-start = ((), (), s32[]{:S(2)}) async-start(), calls=%async_computation.10 | async-start | bytes 1179648 | tf_op jit(solution)/shard_map/reduce_scatter | solution.py:131
  29.6 3.8 copy-start.8
  29.6 8.8 %copy-start.3 = (bf16[128,768]{1,0:T(8,128)(2,1)S(1)}, bf16[128,768]{1,0:T(8,128)(2,1)}, u32[]{:S(2)}) copy-start(bf16[128,768]{1,0:T(8,128)(2,1)} %param.15) | copy-start | bytes 589828
  29.6 10.3 %copy-start.24 = (f32[768]{0:T(1024)S(1)}, f32[768]{0:T(1024)}, u32[]{:S(2)}) copy-start(f32[768]{0:T(1024)} %param.23) | copy-start | bytes 9220
  38.4 4.5 copy-start.16
  38.4 4.5 copy-start.42
  42.9 3.5 copy-start.12
  49.0 21.0 %reduce-scatter.11.cloned.1.call-start = ((), (), s32[]{:S(2)}) async-start(), calls=%async_computation.9 | async-start | bytes 1179648 | tf_op jit(solution)/shard_map/reduce_scatter | solution.py:119
  53.1 60.3 %reduce-scatter.15.cloned.1.call-start = ((), (), s32[]{:S(2)}) async-start(), calls=%async_computation.11 | async-start | bytes 1179648 | tf_op jit(solution)/shard_map/reduce_scatter | solution.py:161
  70.0 5.7 copy-start.11
  76.8 6.0 copy-start.27
  78.5 4.2 copy-start.2
  78.5 4.2 copy-start.18
  78.5 4.2 copy-start.21
  78.5 4.2 copy-start.23
  94.4 140.8 %reduce-scatter.19.cloned.1.call-start = ((), (), s32[]{:S(2)}) async-start(), calls=%async_computation.13 | async-start | bytes 1253376 | tf_op jit(solution)/shard_map/reduce_scatter | solution.py:167
  95.9 278.3 %reduce-scatter.17.cloned.1.call-start = ((), (), s32[]{:S(2)}) async-start(), calls=%async_computation.12 | async-start | bytes 3760128 | tf_op jit(solution)/shard_map/reduce_scatter | solution.py:166
  102.0 414.9 %reduce-scatter.23.cloned.1.call-start = ((), (), s32[]{:S(2)}) async-start(), calls=%async_computation.15 | async-start | bytes 5013504 | tf_op jit(solution)/shard_map/reduce_scatter | solution.py:169
  107.6 552.6 %reduce-scatter.21.cloned.1.call-start = ((), (), s32[]{:S(2)}) async-start(), calls=%async_computation.14 | async-start | bytes 5013504 | tf_op jit(solution)/shard_map/reduce_scatter | solution.py:168
  112.7 5.5 copy-start.35
  112.7 83.3 %copy-start.5 = (f32[128,768]{1,0:T(8,128)S(1)}, f32[128,768]{1,0:T(8,128)}, u32[]{:S(2)}) copy-start(f32[128,768]{1,0:T(8,128)} %copy-done.4) | copy-start | bytes 1179652
  (27 other events, 37.1 us)
Sparse Core Ops, SparseCore 0:
  27.6 10.7 reduce-scatter.8
  49.1 9.2 reduce-scatter.12
  60.7 9.2 reduce-scatter.10
  94.5 9.2 reduce-scatter.14
  109.0 126.1 reduce-scatter.18
  240.7 133.4 reduce-scatter.16
  380.0 136.8 reduce-scatter.22
  522.6 137.5 reduce-scatter.20
